TPU v7x, 32 devices: a whole 2x2x4 slice. The times are simulated.
32 devices in a mesh: grp: 2 (over x), seq: 16 (over z, y, core).
Axes of the slice: x: 2, y: 2, z: 4, core: 2. Of those that a mesh axis runs over, the one named last changes fastest.
Arguments:
- fresh_query: bfloat16 [4096, 4096], P(('grp', 'seq')), parts along dimension 0, may hold values from -80 to 80
- fresh_key: bfloat16 [4096, 4096], P(('grp', 'seq')), parts along dimension 0, may hold values from -4 to 4
- fresh_value: bfloat16 [4096, 4096], P(('grp', 'seq')), parts along dimension 0, may hold values from -4 to 4
- stale_key: bfloat16 [8192, 4096], P('grp', 'seq'), parts along dimension 0, may hold values from -4 to 4
- stale_value: bfloat16 [8192, 4096], P('grp', 'seq'), parts along dimension 0, may hold values from -4 to 4
- patch_start: int32 [2], P('grp'), parts along dimension 0, may hold values from 0 to 2048
- timestep: int32 [2], P('grp'), parts along dimension 0, may hold values from 0 to 34
- gate_table: float32 [35, 4096], replicated, may hold values from -4 to 4
Outputs:
- gated: bfloat16 [4096, 4096], P(('grp', 'seq')), parts along dimension 0
There are 2 independent parts, one for each index of `grp`. A program takes and returns all parts, laid end to end along the dimension named above; an argument that names none is the same for every part. Nothing has to cross between parts.
All inputs are finite; a program needn't handle non-finite values.
Results may differ from a plain program's by a relative error of at most 0.0056.
Values may be sent and summed in bfloat16 or wider, within the bound.
No kernel may reach another device: no remote copies, remote signals or barrier semaphores. Data moves between devices by JAX's collectives and lax.ppermute only.
A program may use at most 64 MiB of HBM per device.

v0:
```python
import jax
import jax.numpy as jnp
from jax import lax
from jax.sharding import PartitionSpec as P

HD = 128


def attend_group(queries, keys, values):
    scores = jnp.dot(queries, keys.T, preferred_element_type=jnp.float32) * HD ** (-0.5)
    row_max = jnp.max(scores, axis=1)
    expo = jnp.exp(scores - row_max[:, None])
    total = jnp.sum(expo, axis=1)
    output = jnp.dot(expo.astype(jnp.bfloat16), values, preferred_element_type=jnp.float32)
    return (row_max, total, output)


def attend_blocks(queries, keys, values):
    all_rows = queries.shape[0]
    block_rows = min(512, all_rows)
    blocks = queries.reshape(all_rows // block_rows, block_rows, queries.shape[1])
    row_max, total, output = lax.map(lambda q_block: attend_group(q_block, keys, values), blocks)
    return (
        row_max.reshape(all_rows),
        total.reshape(all_rows),
        output.reshape(all_rows, values.shape[1]),
    )


def old_partials(queries_all, old_key, old_value, heads_dev):
    results = []
    for head_idx in range(heads_dev):
        cols = slice(head_idx * HD, (head_idx + 1) * HD)
        results.append(
            attend_blocks(queries_all[:, head_idx, :], old_key[:, cols], old_value[:, cols])
        )
    return results


def shards(
    fresh_query, fresh_key, fresh_value, stale_key, stale_value, patch_start, timestep, gate_table
):
    tok_rows = fresh_query.shape[0]
    model_width = fresh_query.shape[1]
    heads_dev = stale_key.shape[1] // HD
    patch_rows = tok_rows * lax.axis_size("seq")
    seq_rows = stale_key.shape[0]
    query_heads = fresh_query.reshape(tok_rows, model_width // HD, HD)
    key_heads = fresh_key.reshape(tok_rows, model_width // HD, HD)
    value_heads = fresh_value.reshape(tok_rows, model_width // HD, HD)
    shift_by = -(patch_start[0] + patch_rows)
    old_key = jnp.roll(stale_key, shift_by, axis=0)[: seq_rows - patch_rows]
    old_value = jnp.roll(stale_value, shift_by, axis=0)[: seq_rows - patch_rows]
    queries_all, keys_all, values_all = (
        lax.all_to_all(query_heads, "seq", split_axis=1, concat_axis=0, tiled=True),
        lax.all_to_all(key_heads, "seq", split_axis=1, concat_axis=0, tiled=True),
        lax.all_to_all(value_heads, "seq", split_axis=1, concat_axis=0, tiled=True),
    )
    old_parts = old_partials(queries_all, old_key, old_value, heads_dev)
    outputs = []
    for head_idx in range(heads_dev):
        max_old, sum_old, out_old = old_parts[head_idx]
        max_new, sum_new, out_new = attend_blocks(
            queries_all[:, head_idx, :], keys_all[:, head_idx, :], values_all[:, head_idx, :]
        )
        top = jnp.maximum(max_old, max_new)
        scale_old = jnp.exp(max_old - top)
        scale_new = jnp.exp(max_new - top)
        numer = scale_old[:, None] * out_old + scale_new[:, None] * out_new
        denom = scale_old * sum_old + scale_new * sum_new
        outputs.append((numer / denom[:, None]).astype(jnp.bfloat16))
    heads_out = jnp.stack(outputs, axis=1)
    back_home = lax.all_to_all(heads_out, "seq", split_axis=0, concat_axis=1, tiled=True)
    attn = back_home.reshape(tok_rows, model_width)
    gate_row = lax.dynamic_slice_in_dim(gate_table, timestep[0], 1, 0)
    return (attn.astype(jnp.float32) * gate_row).astype(jnp.bfloat16)


def solution(mesh):
    return jax.shard_map(
        shards,
        mesh=mesh,
        in_specs=(
            P(("grp", "seq"), None),
            P(("grp", "seq"), None),
            P(("grp", "seq"), None),
            P("grp", "seq"),
            P("grp", "seq"),
            P("grp"),
            P("grp"),
            P(),
        ),
        out_specs=P(("grp", "seq"), None),
        check_vma=False,
    )
```

profile of v0, /device:TPU:11, one launch (start us, length us, event | category | flops | bytes accessed | tf_op | source)
XLA Modules:
  0.0 210.6 jit_solution(3825884178690398125)
XLA Ops:
  0.0 1.7 copy.40
  3.1 6.6 %all-to-all-start = ((bf16[128,32,128]{2,0,1:T(8,128)(2,1)}), bf16[128,32,128]{2,0,1:T(8,128)(2,1)S(1)}, u32[]{:S(2)}, u32[]{:S(2)}) async-start(bf16[128,32,128]{2,0,1:T(8,128)(2,1)} %copy.41), calls=%async_computation | async-start | bytes 2097152 | tf_op jit(solution)/shard_map/all_to_all | solution.py:55
  11.6 2.3 %copy.46 = bf16[128,4096]{0,1:T(8,128)(2,1)} copy(bf16[128,4096]{1,0:T(8,128)(2,1)} %param.20) | data formatting | bytes 2097152 | tf_op args[2]
  13.9 20.7 %all-to-all-done = bf16[128,32,128]{2,0,1:T(8,128)(2,1)S(1)} async-done(((bf16[128,32,128]{2,0,1:T(8,128)(2,1)}), bf16[128,32,128]{2,0,1:T(8,128)(2,1)S(1)}, u32[]{:S(2)}, u32[]{:S(2)}) %all-to-all-start) | async-done | bytes 1048608 | tf_op jit(solution)/shard_map/all_to_all | solution.py:55
  34.6 4.8 %all-to-all-start.1 = ((bf16[128,32,128]{0,2,1:T(8,128)(2,1)}), bf16[128,32,128]{0,2,1:T(8,128)(2,1)}, u32[]{:S(2)}, u32[]{:S(2)}) async-start(bf16[128,32,128]{0,2,1:T(8,128)(2,1)} %bitcast.22), calls=%async_computation.1 | async-start | bytes 2097152 | tf_op jit(solution)/shard_map/all_to_all | solution.py:56
  39.3 4.8 %fusion.68 = (bf16[4096,256]{1,0:T(8,128)(2,1)S(1)}, bf16[4096,256]{1,0:T(8,128)(2,1)S(1)}) fusion(s32[]{:T(128)S(6)} %select_n.17, bf16[4096,256]{1,0:T(8,128)(2,1)} %param.22, bf16[4096,256]{1,0:T(8,128)(2,1)} %param.21), kind=kLoop, calls=%fused_computation.60 | loop fusion | flops 8388608 | bytes 8388612 | tf_op jit(solution)/shard_map/jit(_roll_dynamic)/concatenate | solution.py:53
  46.4 17.9 %all-to-all-done.1 = bf16[128,32,128]{0,2,1:T(8,128)(2,1)} async-done(((bf16[128,32,128]{0,2,1:T(8,128)(2,1)}), bf16[128,32,128]{0,2,1:T(8,128)(2,1)}, u32[]{:S(2)}, u32[]{:S(2)}) %all-to-all-start.1) | async-done | bytes 1048608 | tf_op jit(solution)/shard_map/all_to_all | solution.py:56
  64.4 4.8 %all-to-all-start.2 = ((bf16[128,32,128]{0,2,1:T(8,128)(2,1)}), bf16[128,32,128]{0,2,1:T(8,128)(2,1)}, u32[]{:S(2)}, u32[]{:S(2)}) async-start(bf16[128,32,128]{0,2,1:T(8,128)(2,1)} %bitcast.163), calls=%async_computation.2 | async-start | bytes 2097152 | tf_op jit(solution)/shard_map/all_to_all | solution.py:57
  70.2 13.2 %while.56 = (s32[]{:T(128)}, f32[4,512]{1,0:T(4,128)S(1)}, f32[4,512]{1,0:T(4,128)S(1)}, f32[4,512,128]{2,1,0:T(8,128)}, bf16[4,512,128]{2,1,0:T(8,128)(2,1)S(1)...) while((s32[]{:T(128)}, f32[4,512]{1,0:T(4,128)S(1)}, ...), condition=%wide.region_3.5_spmd, body=%wide.region_0.4_spmd.sunk | while | flops 545258496 | bytes 14041705 | solution.py:22
  83.4 2.4 %copy.45 = bf16[16,128,2,128]{3,1,0,2:T(8,128)(2,1)} copy(bf16[16,128,2,128]{1,3,2,0:T(8,128)(2,1)} %bitcast.25) | data formatting | bytes 2097152 | tf_op jit(solution)/shard_map/all_to_all | solution.py:56
  85.8 8.3 %all-to-all-done.2 = bf16[128,32,128]{0,2,1:T(8,128)(2,1)} async-done(((bf16[128,32,128]{0,2,1:T(8,128)(2,1)}), bf16[128,32,128]{0,2,1:T(8,128)(2,1)}, u32[]{:S(2)}, u32[]{:S(2)}) %all-to-all-start.2) | async-done | bytes 1048608 | tf_op jit(solution)/shard_map/all_to_all | solution.py:57
  94.1 2.3 %copy.48 = bf16[16,128,2,128]{3,1,0,2:T(8,128)(2,1)} copy(bf16[16,128,2,128]{1,3,2,0:T(8,128)(2,1)} %bitcast.31) | data formatting | bytes 2097152 | tf_op jit(solution)/shard_map/all_to_all | solution.py:57
  96.4 2.5 %slice_bitcast_fusion.2 = (bf16[2048,128]{1,0:T(8,128)(2,1)S(1)}, bf16[2048,128]{1,0:T(8,128)(2,1)S(1)}, bf16[2048,128]{1,0:T(8,128)(2,1)S(1)}, bf16[2048,128]{1,0:T(8,128)(2,1)}) fusion(bf16[2048,2,128]{2,0,1:T(8,128)(2,1)} %bitcast.168, bf16[2048,2,128]{2,0,1:T(8,128)(2,1)} %bitcast.167), kind=kLoop, calls=%fused_computation.70 | loop fusion | bytes 4194304 | tf_op jit(solution)/shard_map/squeeze | solution.py:64
  99.9 17.5 %while.57 = (s32[]{:T(128)}, f32[4,512]{1,0:T(4,128)S(1)}, f32[4,512]{1,0:T(4,128)S(1)}, f32[4,512,128]{2,1,0:T(8,128)}, bf16[4,512,128]{2,1,0:T(8,128)(2,1)}, /...) while((s32[]{:T(128)}, f32[4,512]{1,0:T(4,128)S(1)}, ...), condition=%wide.region_7.9_spmd, body=%wide.region_4.8_spmd.sunk | while | flops 545258496 | bytes 14042213 | solution.py:22
  99.9 1.9 multiply_reduce_fusion.9
  104.3 1.9 multiply_reduce_fusion.9
  108.7 1.9 multiply_reduce_fusion.9
  113.1 1.9 multiply_reduce_fusion.9
  118.6 16.7 %while.58 = (s32[]{:T(128)}, f32[4,512]{1,0:T(4,128)S(1)}, f32[4,512]{1,0:T(4,128)S(1)}, f32[4,512,128]{2,1,0:T(8,128)}, bf16[4,512,128]{2,1,0:T(8,128)(2,1)}, /...) while((s32[]{:T(128)}, f32[4,512]{1,0:T(4,128)S(1)}, ...), condition=%wide.region_11.13_spmd, body=%wide.region_8.12_spmd.sunk | while | flops 545258496 | bytes 14042213 | solution.py:22
  122.7 1.7 multiply_reduce_fusion.10
  126.9 1.7 multiply_reduce_fusion.10
  131.1 1.7 multiply_reduce_fusion.10
  135.4 13.9 %while.59 = (s32[]{:T(128)}, f32[4,512]{1,0:T(4,128)S(1)}, f32[4,512]{1,0:T(4,128)S(1)}, f32[4,512,128]{2,1,0:T(8,128)S(1)}, bf16[4,512,128]{2,1,0:T(8,128)(2,1)...) while((s32[]{:T(128)}, f32[4,512]{1,0:T(4,128)S(1)}, ...), condition=%wide.region_15.17_spmd, body=%wide.region_12.16_spmd.sunk | while | flops 545258496 | bytes 14041705 | solution.py:22
  135.4 1.7 multiply_reduce_fusion.11
  145.9 1.7 multiply_reduce_fusion.11
  149.4 10.3 %divide_convert_fusion.1 = bf16[2048,1,128]{2,1,0:T(2,128)(2,1)S(1)} fusion(f32[2048,1,128]{2,1,0:T(1,128)} %bitcast.35, f32[2048,1,128]{2,1,0:T(1,128)} %bitcast.34, f32[2048]{0:T(1024)S(1)} %get-tuple-element.230, f32[2048]{0:T(1024)S(1)} %get-tuple-element.232, f32[2048]{0:T(1024)S(1)} %get-tuple-element.231), kind=kLoop, calls=%fused_computation.67 | loop fusion | flops 1310720 | bytes 2646016 | tf_op jit(solution)/shard_map/convert_element_type | solution.py:71
  159.7 10.2 %divide_convert_fusion = bf16[2048,1,128]{2,1,0:T(2,128)(2,1)S(1)} fusion(f32[2048,1,128]{2,1,0:T(1,128)S(1)} %bitcast.161, f32[2048,1,128]{2,1,0:T(1,128)} %bitcast.39, f32[2048]{0:T(1024)S(1)} %get-tuple-element.233, f32[2048]{0:T(1024)S(1)} %get-tuple-element.235, f32[2048]{0:T(1024)S(1)} %get-tuple-element.234), kind=kLoop, calls=%fused_computation.66 | loop fusion | flops 1310720 | bytes 2646016 | tf_op jit(solution)/shard_map/convert_element_type | solution.py:71
  170.0 3.4 %pad_maximum_fusion = bf16[2048,2,128]{2,1,0:T(2,128)(2,1)} fusion(bf16[2048,1,128]{2,1,0:T(2,128)(2,1)S(1)} %divide_convert_fusion, bf16[2048,1,128]{2,1,0:T(2,128)(2,1)S(1)} %divide_convert_fusion.1), kind=kLoop, calls=%fused_computation.65 | loop fusion | flops 2097152 | bytes 2097152 | tf_op jit(solution)/shard_map/stack | solution.py:72
  173.4 4.8 %all-to-all-start.3 = ((bf16[2048,2,128]{2,1,0:T(2,128)(2,1)}), bf16[2048,2,128]{2,1,0:T(2,128)(2,1)S(1)}, u32[]{:S(2)}, u32[]{:S(2)}) async-start(bf16[2048,2,128]{2,1,0:T(2,128)(2,1)} %pad_maximum_fusion), calls=%async_computation.3 | async-start | bytes 2097152 | tf_op jit(solution)/shard_map/all_to_all | solution.py:73
  178.9 24.2 %all-to-all-done.3 = bf16[2048,2,128]{2,1,0:T(2,128)(2,1)S(1)} async-done(((bf16[2048,2,128]{2,1,0:T(2,128)(2,1)}), bf16[2048,2,128]{2,1,0:T(2,128)(2,1)S(1)}, u32[]{:S(2)}, u32[]{:S(2)}) %all-to-all-start.3) | async-done | bytes 1048608 | tf_op jit(solution)/shard_map/all_to_all | solution.py:73
  204.8 1.9 copy.50
  208.4 2.3 %copy.51 = bf16[128,4096]{1,0:T(8,128)(2,1)} copy(bf16[128,4096]{0,1:T(8,128)(2,1)} %fusion.70) | data formatting | bytes 2097152 | tf_op jit(solution)/shard_map/convert_element_type | solution.py:76
  (113 shorter events, 56.4 us)
Async XLA Ops:
  0.0 178.8 %copy-start = (f32[35,4096]{1,0:T(8,128)S(1)}, f32[35,4096]{1,0:T(8,128)}, u32[]{:S(2)}) copy-start(f32[35,4096]{1,0:T(8,128)} %param.25) | copy-start | bytes 1720324
  0.0 10.3 %copy-start.4 = (bf16[128,4096]{1,0:T(8,128)(2,1)S(1)}, bf16[128,4096]{1,0:T(8,128)(2,1)}, u32[]{:S(2)}) copy-start(bf16[128,4096]{1,0:T(8,128)(2,1)} %param.19) | copy-start | bytes 3145732
  3.1 31.5 %all-to-all-start = ((bf16[128,32,128]{2,0,1:T(8,128)(2,1)}), bf16[128,32,128]{2,0,1:T(8,128)(2,1)S(1)}, u32[]{:S(2)}, u32[]{:S(2)}) async-start(bf16[128,32,128]{2,0,1:T(8,128)(2,1)} %copy.41), calls=%async_computation | async-start | bytes 2097152 | tf_op jit(solution)/shard_map/all_to_all | solution.py:55
  34.6 9.6 %copy-start.2 = (bf16[128,32,128]{2,0,1:T(8,128)(2,1)}, bf16[128,32,128]{2,0,1:T(8,128)(2,1)S(1)}, u32[]{:S(2)}) copy-start(bf16[128,32,128]{2,0,1:T(8,128)(2,1)S(1)} %all-to-all-done) | copy-start | bytes 3145732
  34.6 29.8 %all-to-all-start.1 = ((bf16[128,32,128]{0,2,1:T(8,128)(2,1)}), bf16[128,32,128]{0,2,1:T(8,128)(2,1)}, u32[]{:S(2)}, u32[]{:S(2)}) async-start(bf16[128,32,128]{0,2,1:T(8,128)(2,1)} %bitcast.22), calls=%async_computation.1 | async-start | bytes 2097152 | tf_op jit(solution)/shard_map/all_to_all | solution.py:56
  44.2 1.2 copy-start.3
  64.4 29.8 %all-to-all-start.2 = ((bf16[128,32,128]{0,2,1:T(8,128)(2,1)}), bf16[128,32,128]{0,2,1:T(8,128)(2,1)}, u32[]{:S(2)}, u32[]{:S(2)}) async-start(bf16[128,32,128]{0,2,1:T(8,128)(2,1)} %bitcast.163), calls=%async_computation.2 | async-start | bytes 2097152 | tf_op jit(solution)/shard_map/all_to_all | solution.py:57
  83.3 13.1 %copy-start.1 = (bf16[4,512,128]{2,1,0:T(8,128)(2,1)}, bf16[4,512,128]{2,1,0:T(8,128)(2,1)S(1)}, u32[]{:S(2)}) copy-start(bf16[4,512,128]{2,1,0:T(8,128)(2,1)S(1)} %get-tuple-element.555) | copy-start | bytes 1572868
  173.4 29.7 %all-to-all-start.3 = ((bf16[2048,2,128]{2,1,0:T(2,128)(2,1)}), bf16[2048,2,128]{2,1,0:T(2,128)(2,1)S(1)}, u32[]{:S(2)}, u32[]{:S(2)}) async-start(bf16[2048,2,128]{2,1,0:T(2,128)(2,1)} %pad_maximum_fusion), calls=%async_computation.3 | async-start | bytes 2097152 | tf_op jit(solution)/shard_map/all_to_all | solution.py:73
where the time goes:
time: 212 us; the launch traced here: 211 us
  waiting for transfers between devices  71.2 us (34%)
  matrix products  46.4 us (22%)
  other arithmetic  45.1 us (21%)
  local copies, waits for them, and re-layouts  25.2 us (12%)
  starting transfers between devices  20.9 us (10%)
    dot_general x16, matrix products, attend_group(): jnp.dot(queries, keys.T, preferred_element_type=jnp.float32) * HD ** (-0.5)  24.3 us
    all_to_all x1, waiting for transfers between devices, shards(): lax.all_to_all(heads_out, 'seq', split_axis=0, concat_axis=1, tiled=True)  24.2 us
    dot_general x16, matrix products, attend_group(): jnp.dot(expo.astype(jnp.bfloat16), values, preferred_element_type=jnp.flo...  22.1 us
    all_to_all x1, waiting for transfers between devices, shards(): lax.all_to_all(query_heads, 'seq', split_axis=1, concat_axis=0, tiled=True)  20.7 us
    convert_element_type x2, other arithmetic, shards(): outputs.append((numer / denom[:, None]).astype(jnp.bfloat16))  20.5 us
    all_to_all x1, waiting for transfers between devices, shards(): lax.all_to_all(key_heads, 'seq', split_axis=1, concat_axis=0, tiled=True)  17.9 us
    reduce_sum x16, other arithmetic, attend_group(): total = jnp.sum(expo, axis=1)  13 us
    all_to_all x1, waiting for transfers between devices, shards(): lax.all_to_all(value_heads, 'seq', split_axis=1, concat_axis=0, tiled=True)  8.33 us
  transfers between devices with their start and end apart: 4, of which 4 were waited for; matrix products, arithmetic and copies ran while one was open for 12% of the time, Pallas kernels for 0%

commit v1 on v0

--- a/solution.py
+++ b/solution.py
@@ -70,7 +70,10 @@
         denom = scale_old * sum_old + scale_new * sum_new
         outputs.append((numer / denom[:, None]).astype(jnp.bfloat16))
     heads_out = jnp.stack(outputs, axis=1)
-    back_home = lax.all_to_all(heads_out, "seq", split_axis=0, concat_axis=1, tiled=True)
+    back_home = jnp.concatenate(
+        lax.all_to_all(jnp.stack(jnp.split(heads_out, lax.psum(1, "seq"), axis=0)), "seq", 0, 0),
+        axis=1,
+    )
     attn = back_home.reshape(tok_rows, model_width)
     gate_row = lax.dynamic_slice_in_dim(gate_table, timestep[0], 1, 0)
     return (attn.astype(jnp.float32) * gate_row).astype(jnp.bfloat16)

time: 212 us -> 216 us (1.019)
  other arithmetic: 45.1 us -> 51.9 us
  local copies, waits for them, and re-layouts: 25.2 us -> 23 us
    unnamed x0 -> x15, other arithmetic: none -> 11.7 us
    convert_element_type x2 -> x1, local copies, waits for them, and re-layouts: 4.19 us -> 1.31 us  [shards(): return (attn.astype(jnp.float32) * gate_row).astype(jnp.bfloat16)]
    another operation x1, other arithmetic: 3.43 us -> 0.78 us  [shards(): jnp.stack(jnp.split(heads_out, lax.psum(1, 'seq'), axis=0))]
    convert_element_type x2 -> x1, other arithmetic: 3.21 us -> 0.71 us  [shards(): return (attn.astype(jnp.float32) * gate_row).astype(jnp.bfloat16)]
where the time goes in v1:
time: 216 us; the launch traced here: 215 us
  waiting for transfers between devices  71.2 us (33%)
  other arithmetic  51.9 us (24%)
  matrix products  46.4 us (21%)
  local copies, waits for them, and re-layouts  23 us (11%)
  starting transfers between devices  20.9 us (10%)
    dot_general x16, matrix products, attend_group(): jnp.dot(queries, keys.T, preferred_element_type=jnp.float32) * HD ** (-0.5)  24.3 us
    all_to_all x1, waiting for transfers between devices, shards(): lax.all_to_all(jnp.stack(jnp.split(heads_out, lax.psum(1, 'seq'), axis=0)...  24.2 us
    dot_general x16, matrix products, attend_group(): jnp.dot(expo.astype(jnp.bfloat16), values, preferred_element_type=jnp.flo...  22.1 us
    convert_element_type x2, other arithmetic, shards(): outputs.append((numer / denom[:, None]).astype(jnp.bfloat16))  20.8 us
    all_to_all x1, waiting for transfers between devices, shards(): lax.all_to_all(query_heads, 'seq', split_axis=1, concat_axis=0, tiled=True)  20.7 us
    all_to_all x1, waiting for transfers between devices, shards(): lax.all_to_all(key_heads, 'seq', split_axis=1, concat_axis=0, tiled=True)  17.9 us
    reduce_sum x16, other arithmetic, attend_group(): total = jnp.sum(expo, axis=1)  13 us
    unnamed x15, other arithmetic  11.7 us
  transfers between devices with their start and end apart: 4, of which 4 were waited for; matrix products, arithmetic and copies ran while one was open for 12% of the time, Pallas kernels for 0%

profile of v1, /device:TPU:11, one launch (start us, length us, event | category | flops | bytes accessed | tf_op | source)
XLA Modules:
  0.0 215.3 jit_solution(14512086072215667148)
XLA Ops:
  0.0 1.7 copy.91
  3.1 6.6 %all-to-all-start = ((bf16[128,32,128]{2,0,1:T(8,128)(2,1)}), bf16[128,32,128]{2,0,1:T(8,128)(2,1)S(1)}, u32[]{:S(2)}, u32[]{:S(2)}) async-start(bf16[128,32,128]{2,0,1:T(8,128)(2,1)} %copy.92), calls=%async_computation | async-start | bytes 2097152 | tf_op jit(solution)/shard_map/all_to_all | solution.py:55
  11.6 2.3 %copy.97 = bf16[128,4096]{0,1:T(8,128)(2,1)} copy(bf16[128,4096]{1,0:T(8,128)(2,1)} %param.20) | data formatting | bytes 2097152 | tf_op args[2]
  13.9 20.7 %all-to-all-done = bf16[128,32,128]{2,0,1:T(8,128)(2,1)S(1)} async-done(((bf16[128,32,128]{2,0,1:T(8,128)(2,1)}), bf16[128,32,128]{2,0,1:T(8,128)(2,1)S(1)}, u32[]{:S(2)}, u32[]{:S(2)}) %all-to-all-start) | async-done | bytes 1048608 | tf_op jit(solution)/shard_map/all_to_all | solution.py:55
  34.6 4.8 %all-to-all-start.1 = ((bf16[128,32,128]{0,2,1:T(8,128)(2,1)}), bf16[128,32,128]{0,2,1:T(8,128)(2,1)}, u32[]{:S(2)}, u32[]{:S(2)}) async-start(bf16[128,32,128]{0,2,1:T(8,128)(2,1)} %bitcast.22), calls=%async_computation.1 | async-start | bytes 2097152 | tf_op jit(solution)/shard_map/all_to_all | solution.py:56
  39.3 4.8 %fusion.68 = (bf16[4096,256]{1,0:T(8,128)(2,1)S(1)}, bf16[4096,256]{1,0:T(8,128)(2,1)S(1)}) fusion(s32[]{:T(128)S(6)} %select_n.17, bf16[4096,256]{1,0:T(8,128)(2,1)} %param.22, bf16[4096,256]{1,0:T(8,128)(2,1)} %param.21), kind=kLoop, calls=%fused_computation.60 | loop fusion | flops 8388608 | bytes 8388612 | tf_op jit(solution)/shard_map/jit(_roll_dynamic)/concatenate | solution.py:53
  46.4 17.9 %all-to-all-done.1 = bf16[128,32,128]{0,2,1:T(8,128)(2,1)} async-done(((bf16[128,32,128]{0,2,1:T(8,128)(2,1)}), bf16[128,32,128]{0,2,1:T(8,128)(2,1)}, u32[]{:S(2)}, u32[]{:S(2)}) %all-to-all-start.1) | async-done | bytes 1048608 | tf_op jit(solution)/shard_map/all_to_all | solution.py:56
  64.4 4.8 %all-to-all-start.2 = ((bf16[128,32,128]{0,2,1:T(8,128)(2,1)}), bf16[128,32,128]{0,2,1:T(8,128)(2,1)}, u32[]{:S(2)}, u32[]{:S(2)}) async-start(bf16[128,32,128]{0,2,1:T(8,128)(2,1)} %bitcast.224), calls=%async_computation.2 | async-start | bytes 2097152 | tf_op jit(solution)/shard_map/all_to_all | solution.py:57
  70.2 13.2 %while.56 = (s32[]{:T(128)}, f32[4,512]{1,0:T(4,128)S(1)}, f32[4,512]{1,0:T(4,128)S(1)}, f32[4,512,128]{2,1,0:T(8,128)}, bf16[4,512,128]{2,1,0:T(8,128)(2,1)S(1)...) while((s32[]{:T(128)}, f32[4,512]{1,0:T(4,128)S(1)}, ...), condition=%wide.region_3.5_spmd, body=%wide.region_0.4_spmd.sunk | while | flops 545258496 | bytes 14041705 | solution.py:22
  83.4 2.4 %copy.96 = bf16[16,128,2,128]{3,1,0,2:T(8,128)(2,1)} copy(bf16[16,128,2,128]{1,3,2,0:T(8,128)(2,1)} %bitcast.25) | data formatting | bytes 2097152 | tf_op jit(solution)/shard_map/all_to_all | solution.py:56
  85.8 8.3 %all-to-all-done.2 = bf16[128,32,128]{0,2,1:T(8,128)(2,1)} async-done(((bf16[128,32,128]{0,2,1:T(8,128)(2,1)}), bf16[128,32,128]{0,2,1:T(8,128)(2,1)}, u32[]{:S(2)}, u32[]{:S(2)}) %all-to-all-start.2) | async-done | bytes 1048608 | tf_op jit(solution)/shard_map/all_to_all | solution.py:57
  94.1 2.3 %copy.99 = bf16[16,128,2,128]{3,1,0,2:T(8,128)(2,1)} copy(bf16[16,128,2,128]{1,3,2,0:T(8,128)(2,1)} %bitcast.31) | data formatting | bytes 2097152 | tf_op jit(solution)/shard_map/all_to_all | solution.py:57
  96.4 2.5 %slice_bitcast_fusion.2 = (bf16[2048,128]{1,0:T(8,128)(2,1)S(1)}, bf16[2048,128]{1,0:T(8,128)(2,1)S(1)}, bf16[2048,128]{1,0:T(8,128)(2,1)S(1)}, bf16[2048,128]{1,0:T(8,128)(2,1)}) fusion(bf16[2048,2,128]{2,0,1:T(8,128)(2,1)} %bitcast.229, bf16[2048,2,128]{2,0,1:T(8,128)(2,1)} %bitcast.228), kind=kLoop, calls=%fused_computation.68 | loop fusion | bytes 4194304 | tf_op jit(solution)/shard_map/squeeze | solution.py:64
  99.9 17.5 %while.57 = (s32[]{:T(128)}, f32[4,512]{1,0:T(4,128)S(1)}, f32[4,512]{1,0:T(4,128)S(1)}, f32[4,512,128]{2,1,0:T(8,128)}, bf16[4,512,128]{2,1,0:T(8,128)(2,1)}, /...) while((s32[]{:T(128)}, f32[4,512]{1,0:T(4,128)S(1)}, ...), condition=%wide.region_7.9_spmd, body=%wide.region_4.8_spmd.sunk | while | flops 545258496 | bytes 14042213 | solution.py:22
  99.9 1.9 multiply_reduce_fusion.9
  104.3 1.9 multiply_reduce_fusion.9
  108.7 1.9 multiply_reduce_fusion.9
  113.1 1.9 multiply_reduce_fusion.9
  118.6 16.7 %while.58 = (s32[]{:T(128)}, f32[4,512]{1,0:T(4,128)S(1)}, f32[4,512]{1,0:T(4,128)S(1)}, f32[4,512,128]{2,1,0:T(8,128)}, bf16[4,512,128]{2,1,0:T(8,128)(2,1)}, /...) while((s32[]{:T(128)}, f32[4,512]{1,0:T(4,128)S(1)}, ...), condition=%wide.region_11.13_spmd, body=%wide.region_8.12_spmd.sunk | while | flops 545258496 | bytes 14042213 | solution.py:22
  118.6 1.7 multiply_reduce_fusion.10
  122.7 1.7 multiply_reduce_fusion.10
  126.9 1.7 multiply_reduce_fusion.10
  131.1 1.7 multiply_reduce_fusion.10
  135.4 13.9 %while.59 = (s32[]{:T(128)}, f32[4,512]{1,0:T(4,128)S(1)}, f32[4,512]{1,0:T(4,128)S(1)}, f32[4,512,128]{2,1,0:T(8,128)S(1)}, bf16[4,512,128]{2,1,0:T(8,128)(2,1)...) while((s32[]{:T(128)}, f32[4,512]{1,0:T(4,128)S(1)}, ...), condition=%wide.region_15.17_spmd, body=%wide.region_12.16_spmd.sunk | while | flops 545258496 | bytes 14041705 | solution.py:22
  135.4 1.7 multiply_reduce_fusion.11
  138.9 1.7 multiply_reduce_fusion.11
  142.4 1.7 multiply_reduce_fusion.11
  145.9 1.7 multiply_reduce_fusion.11
  149.4 10.3 %divide_convert_fusion.1 = bf16[2048,1,128]{2,1,0:T(2,128)(2,1)S(1)} fusion(f32[2048,1,128]{2,1,0:T(1,128)} %bitcast.35, f32[2048,1,128]{2,1,0:T(1,128)} %bitcast.34, f32[2048]{0:T(1024)S(1)} %get-tuple-element.230, f32[2048]{0:T(1024)S(1)} %get-tuple-element.232, f32[2048]{0:T(1024)S(1)} %get-tuple-element.231), kind=kLoop, calls=%fused_computation.65 | loop fusion | flops 1310720 | bytes 2646016 | tf_op jit(solution)/shard_map/convert_element_type | solution.py:71
  159.7 10.4 %divide_convert_fusion = bf16[2048,1,128]{2,1,0:T(2,128)(2,1)S(1)} fusion(f32[2048,1,128]{2,1,0:T(1,128)S(1)} %bitcast.223, f32[2048,1,128]{2,1,0:T(1,128)} %bitcast.39, f32[2048]{0:T(1024)S(1)} %get-tuple-element.233, f32[2048]{0:T(1024)S(1)} %get-tuple-element.235, f32[2048]{0:T(1024)S(1)} %get-tuple-element.234), kind=kLoop, calls=%fused_computation.64 | loop fusion | flops 1310720 | bytes 2646016 | tf_op jit(solution)/shard_map/convert_element_type | solution.py:71
  182.7 4.8 %all-to-all-start.3 = ((bf16[16,128,2,128]{3,2,1,0:T(2,128)(2,1)}), bf16[16,128,2,128]{3,2,1,0:T(2,128)(2,1)S(1)}, u32[]{:S(2)}, u32[]{:S(2)}) async-start(bf16[16,128,2,128]{3,2,1,0:T(2,128)(2,1)} %fusion.72), calls=%async_computation.3 | async-start | bytes 2097152 | tf_op jit(solution)/shard_map/all_to_all | solution.py:74
  188.2 24.2 %all-to-all-done.3 = bf16[16,128,2,128]{3,2,1,0:T(2,128)(2,1)S(1)} async-done(((bf16[16,128,2,128]{3,2,1,0:T(2,128)(2,1)}), bf16[16,128,2,128]{3,2,1,0:T(2,128)(2,1)S(1)}, u32[]{:S(2)}, u32[]{:S(2)}) %all-to-all-start.3) | async-done | bytes 1048608 | tf_op jit(solution)/shard_map/all_to_all | solution.py:74
  (126 shorter events, 63.4 us)
Async XLA Ops:
  0.0 188.1 %copy-start = (f32[35,4096]{1,0:T(8,128)S(1)}, f32[35,4096]{1,0:T(8,128)}, u32[]{:S(2)}) copy-start(f32[35,4096]{1,0:T(8,128)} %param.25) | copy-start | bytes 1720324
  0.0 10.3 %copy-start.4 = (bf16[128,4096]{1,0:T(8,128)(2,1)S(1)}, bf16[128,4096]{1,0:T(8,128)(2,1)}, u32[]{:S(2)}) copy-start(bf16[128,4096]{1,0:T(8,128)(2,1)} %param.19) | copy-start | bytes 3145732
  3.1 31.5 %all-to-all-start = ((bf16[128,32,128]{2,0,1:T(8,128)(2,1)}), bf16[128,32,128]{2,0,1:T(8,128)(2,1)S(1)}, u32[]{:S(2)}, u32[]{:S(2)}) async-start(bf16[128,32,128]{2,0,1:T(8,128)(2,1)} %copy.92), calls=%async_computation | async-start | bytes 2097152 | tf_op jit(solution)/shard_map/all_to_all | solution.py:55
  34.6 9.6 %copy-start.2 = (bf16[128,32,128]{2,0,1:T(8,128)(2,1)}, bf16[128,32,128]{2,0,1:T(8,128)(2,1)S(1)}, u32[]{:S(2)}) copy-start(bf16[128,32,128]{2,0,1:T(8,128)(2,1)S(1)} %all-to-all-done) | copy-start | bytes 3145732
  34.6 29.8 %all-to-all-start.1 = ((bf16[128,32,128]{0,2,1:T(8,128)(2,1)}), bf16[128,32,128]{0,2,1:T(8,128)(2,1)}, u32[]{:S(2)}, u32[]{:S(2)}) async-start(bf16[128,32,128]{0,2,1:T(8,128)(2,1)} %bitcast.22), calls=%async_computation.1 | async-start | bytes 2097152 | tf_op jit(solution)/shard_map/all_to_all | solution.py:56
  44.2 1.2 copy-start.3
  64.4 29.8 %all-to-all-start.2 = ((bf16[128,32,128]{0,2,1:T(8,128)(2,1)}), bf16[128,32,128]{0,2,1:T(8,128)(2,1)}, u32[]{:S(2)}, u32[]{:S(2)}) async-start(bf16[128,32,128]{0,2,1:T(8,128)(2,1)} %bitcast.224), calls=%async_computation.2 | async-start | bytes 2097152 | tf_op jit(solution)/shard_map/all_to_all | solution.py:57
  83.3 13.1 %copy-start.1 = (bf16[4,512,128]{2,1,0:T(8,128)(2,1)}, bf16[4,512,128]{2,1,0:T(8,128)(2,1)S(1)}, u32[]{:S(2)}) copy-start(bf16[4,512,128]{2,1,0:T(8,128)(2,1)S(1)} %get-tuple-element.555) | copy-start | bytes 1572868
  182.7 29.7 %all-to-all-start.3 = ((bf16[16,128,2,128]{3,2,1,0:T(2,128)(2,1)}), bf16[16,128,2,128]{3,2,1,0:T(2,128)(2,1)S(1)}, u32[]{:S(2)}, u32[]{:S(2)}) async-start(bf16[16,128,2,128]{3,2,1,0:T(2,128)(2,1)} %fusion.72), calls=%async_computation.3 | async-start | bytes 2097152 | tf_op jit(solution)/shard_map/all_to_all | solution.py:74
